TPU v7x, 256 devices: a whole 4x4x8 slice. The times are simulated.
256 devices in a mesh: tm: 32 (over y, z), space: 8 (over x, core).
Axes of the slice: x: 4, y: 4, z: 8, core: 2. Of those that a mesh axis runs over, the one named last changes fastest.
Arguments:
- inverse_factor: bfloat16 [2, 32, 4096, 4096], P(None, 'tm', 'space'), may hold values from -1.5 to 1.5, as said below
- tile_mask: int32 [32, 32], replicated, may hold values 0 or 1
- carry_rate: float32 [32, 4096, 2], P('tm', 'space'), may hold values from 0 to 1
- right_side: float32 [32, 4096, 2, 128], P('tm', 'space'), may hold values from -1.5 to 1.5
- arrow_rows: bfloat16 [32, 4096, 2, 512], P('tm', 'space'), may hold values from -0.0625 to 0.0625
- fixed_rhs: float32 [2, 512, 128], P(None, ('tm', 'space')), may hold values from -6 to 6
- tip_factor: bfloat16 [2, 512, 512], replicated, may hold values from -1 to 1, as said below
Outputs:
- solution: float32 [32, 4096, 2, 128], P('tm', 'space')
- fixed_solution: float32 [2, 512, 128], P(None, ('tm', 'space'))
Inputs may be any that keep to these rules, and one draw needn't show every extreme that they name: `tile_mask`: 1 marks a tile that may be nonzero. `inverse_factor`: only entries on or below the diagonal are read. `tip_factor`: only entries on or below the diagonal are read.
All inputs are finite; a program needn't handle non-finite values.
Results may differ from a plain program's by a relative error of at most 0.022.
Values may be sent and summed in bfloat16 or wider, within the bound.
No kernel may reach another device: no remote copies, remote signals or barrier semaphores. Data moves between devices by JAX's collectives and lax.ppermute only.
A program may use at most 320 MiB of HBM per device.

v0:
```python
import jax
import jax.numpy as jnp
from jax import lax
from jax.sharding import PartitionSpec as P

TILE = 128


def carried_in(shard, axis, join, neutral, backward):
    count = lax.axis_size(axis)
    place = lax.axis_index(axis)
    ahead = count - 1 - place if backward else place
    gathered = jax.tree.map(
        lambda a, kind: lax.all_gather(a.astype(kind), axis), shard, (jnp.bfloat16, jnp.bfloat16)
    )
    state = jax.tree.map(lambda a, e: jnp.zeros_like(a) + jnp.asarray(e, a.dtype), shard, neutral)

    def one(turn, state):
        source = count - 1 - turn if backward else turn
        return join(
            state,
            jax.tree.map(
                lambda a, own: lax.dynamic_index_in_dim(a, source, 0, False).astype(own.dtype),
                gathered,
                shard,
            ),
        )

    return lax.fori_loop(0, ahead, one, state)


def combine(earlier, latter):
    rate_new = latter[0] * earlier[0]
    rest = tuple(
        (value_l + latter[0] * value_e for value_l, value_e in zip(latter[1:], earlier[1:]))
    )
    return (rate_new,) + rest


def tile_keep(tile_table, row_start, row_total, col_total):
    tile_count = tile_table.shape[0]
    tile_ids = jnp.arange(tile_count, dtype=jnp.int32)
    row_index = row_start + jnp.arange(row_total, dtype=jnp.int32)
    col_index = jnp.arange(col_total, dtype=jnp.int32)
    row_onehot = (row_index[:, None] // TILE == tile_ids[None, :]).astype(jnp.float32)
    col_onehot = (col_index[:, None] // TILE == tile_ids[None, :]).astype(jnp.float32)
    marked = jnp.dot(jnp.dot(row_onehot, tile_table.astype(jnp.float32)), col_onehot.T)
    return (marked > 0.5) & (row_index[:, None] >= col_index[None, :])


def on_device(inverse_factor, tile_mask, carry_rate, right_side, arrow_rows, fixed_rhs, tip_factor):
    row_count = right_side.shape[1]
    node_total = inverse_factor.shape[3]
    row_start = lax.axis_index("space") * row_count
    tile_table = jnp.maximum(tile_mask, jnp.eye(tile_mask.shape[0], dtype=jnp.int32))
    weights = inverse_factor[:, 0]
    bf_zero = jnp.zeros((), jnp.bfloat16)
    rate_col = carry_rate[0][:, :, None]
    source = right_side[0]
    unit_rate = jnp.ones_like(rate_col)
    earlier_sum = carried_in(
        (rate_col, source), "tm", combine, (unit_rate, jnp.zeros_like(source)), False
    )
    forward = source + rate_col * earlier_sum[1]
    forward_b = forward.astype(jnp.bfloat16)
    row_keep = tile_keep(tile_table, row_start, row_count, node_total)
    masked_rows = jnp.where(row_keep[None], weights, bf_zero)
    block = masked_rows
    inner_rows = jnp.einsum(
        "hrn,nhk->rhk",
        block,
        lax.all_gather(forward_b, "space", axis=0, tiled=True),
        preferred_element_type=jnp.float32,
    ).astype(jnp.bfloat16)
    block = masked_rows
    scaled = lax.psum_scatter(
        jnp.einsum("hrn,rhk->nhk", block, inner_rows, preferred_element_type=jnp.float32).astype(
            jnp.bfloat16
        ),
        "space",
        scatter_dimension=0,
        tiled=True,
    ).astype(jnp.float32)
    arrow_part = arrow_rows[0]
    coupling = jnp.einsum("rhf,rhk->hfk", arrow_part, forward_b, preferred_element_type=jnp.float32)
    share_rows = fixed_rhs.shape[1]
    share_start = lax.axis_index(("tm", "space")) * share_rows
    contrib = -coupling
    own_part = lax.dynamic_slice_in_dim(contrib, share_start, share_rows, 1) + fixed_rhs
    contrib = lax.dynamic_update_slice_in_dim(contrib, own_part, share_start, 1)
    fixed_forward = lax.psum(contrib, ("tm", "space")).astype(jnp.bfloat16)
    fixed_total = tip_factor.shape[1]
    fixed_index = jnp.arange(fixed_total, dtype=jnp.int32)
    lower_tri = fixed_index[:, None] >= fixed_index[None, :]
    tip_lower = jnp.where(lower_tri[None], tip_factor, bf_zero)
    tip_inner = jnp.einsum(
        "hij,hjk->hik", tip_lower, fixed_forward, preferred_element_type=jnp.float32
    ).astype(jnp.bfloat16)
    fixed_solution = jnp.einsum(
        "hij,hik->hjk", tip_lower, tip_inner, preferred_element_type=jnp.float32
    )
    fixed_own = lax.dynamic_slice_in_dim(fixed_solution, share_start, share_rows, 1)
    fixed_b = fixed_solution.astype(jnp.bfloat16)
    carried = scaled - jnp.einsum(
        "rhf,hfk->rhk", arrow_part, fixed_b, preferred_element_type=jnp.float32
    )
    following = carried_in(
        (rate_col, rate_col * carried), "tm", combine, (unit_rate, jnp.zeros_like(carried)), True
    )
    solution = carried + following[1]
    return (solution[None], fixed_own)


def solution(mesh):
    placed = (
        P(None, "tm", "space", None),
        P(),
        P("tm", "space", None),
        P("tm", "space", None, None),
        P("tm", "space", None, None),
        P(None, ("tm", "space"), None),
        P(),
    )
    return jax.shard_map(
        on_device,
        mesh=mesh,
        in_specs=placed,
        out_specs=(P("tm", "space", None, None), P(None, ("tm", "space"), None)),
        check_vma=False,
    )
```

profile of v0, /device:TPU:2, one launch (start us, length us, event | category | flops | bytes accessed | tf_op | source)
XLA Modules:
  0.0 596.0 jit_solution(12626880782622736189)
XLA Ops:
  7.2 1.9 copy.62
  9.2 1.2 copy.34
  11.1 52.1 %all-gather = bf16[32,512,2]{1,2,0:T(2,128)(2,1)S(1)} all-gather(bf16[1,512,2]{1,2,0:T(2,128)(2,1)S(1)} %convert_element_type.103), channel_id=2, replica_groups=mesh['tm'=32,'space'=8] {'tm'}, dimensions={0}, use_global_device_ids=true | all-gather | bytes 67584 | tf_op jit(solution)/shard_map/all_gather | solution.py:14
  63.2 3.3 copy.37
  66.6 46.1 %all-gather.6.cloned.1.call-done = bf16[32,512,2,128]{3,1,2,0:T(8,128)(2,1)} async-done(((bf16[1,512,2,128]{3,1,2,0:T(8,128)(2,1)}), bf16[32,512,2,128]{3,1,2,0:T(8,128)(2,1)}) %all-gather.6.cloned.1.call-update) | async-done | bytes 8388624 | tf_op jit(solution)/shard_map/all_gather | solution.py:14
  114.4 4.2 fusion
  118.6 154.2 %all-gather.8.cloned.1.call-done = bf16[4096,2,128]{0,2,1:T(8,128)(2,1)} async-done(((bf16[512,2,128]{0,2,1:T(8,128)(2,1)}), bf16[4096,2,128]{0,2,1:T(8,128)(2,1)}) %all-gather.8.cloned.1.call-update) | async-done | bytes 2097168 | tf_op jit(solution)/shard_map/all_gather | solution.py:72
  272.7 13.2 %fusion.4 = bf16[4096,2,128]{0,2,1:T(8,128)(2,1)} fusion(bf16[2,1,512,4096]{3,2,1,0:T(8,128)(2,1)} %param.11, pred[512,4096]{1,0:T(8,128)(4,1)} %fusion, bf16[4096,2,128]{0,2,1:T(8,128)(2,1)} %all-gather.8.cloned.1.call-done), kind=kOutput, calls=%fused_computation.12 | convolution fusion | flops 2157051904 | bytes 14680064 | tf_op jit(solution)/shard_map/hrn,rhk->nhk/dot_general | solution.py:77
  286.7 1.1 dynamic_update_slice.3
  287.8 78.9 %all-reduce.1 = bf16[2,512,128]{1,2,0:T(8,128)(2,1)S(1)} all-reduce(f32[2,512,128]{1,2,0:T(8,128)S(1)} %dynamic_update_slice.3), channel_id=1, replica_groups=mesh['tm'=32,'space'=8] {'tm','space'}, use_global_device_ids=true, to_apply=%region_3.4 | all-reduce | flops 131072 | bytes 786432 | tf_op jit(solution)/shard_map/psum | solution.py:91
  366.7 2.3 fusion.9
  369.0 2.1 multiply_convert_fusion
  371.8 102.9 %all-gather.10.cloned.1.call-done = bf16[16384,2,128]{0,2,1:T(8,128)(2,1)} async-done(((bf16[512,2,128]{0,2,1:T(8,128)(2,1)}), bf16[16384,2,128]{0,2,1:T(8,128)(2,1)}) %all-gather.10.cloned.1.call-update) | async-done | bytes 8388624 | tf_op jit(solution)/shard_map/all_gather | solution.py:14
  474.7 21.1 %copy.52 = bf16[16384,2,128]{2,1,0:T(2,128)(2,1)} copy(bf16[16384,2,128]{0,2,1:T(8,128)(2,1)} %all-gather.10.cloned.1.call-done) | data formatting | bytes 16777216 | tf_op jit(solution)/shard_map/while | solution.py:29
  495.9 92.2 %while.27 = (s32[]{:T(128)}, f32[512,2,128]{2,1,0:T(2,128)S(1)}, s32[]{:T(128)}, bf16[32,512,2,128]{3,2,1,0:T(2,128)(2,1)}, bf16[32,512,2,1]{2,1,3,0:T(8,128)(2,...) while((s32[]{:T(128)}, f32[512,2,128]{2,1,0:T(2,128)S(1)}, s32[]{:T(128)}, ...), condition=%wide.region_5.6_spmd, body=%wide.region_4.5_spmd.sunk | while | flops 394246 | bytes 1321107 | solution.py:29
  495.9 0.9 bitcast_convert_fusion.5
  496.9 2.0 convert_add_fusion.5
  498.9 0.9 bitcast_convert_fusion.5
  499.8 2.0 convert_add_fusion.5
  502.8 2.0 convert_add_fusion.5
  505.8 2.0 convert_add_fusion.5
  507.8 0.9 bitcast_convert_fusion.5
  508.8 2.0 convert_add_fusion.5
  510.8 0.9 bitcast_convert_fusion.5
  511.7 2.0 convert_add_fusion.5
  513.8 0.9 bitcast_convert_fusion.5
  514.7 2.0 convert_add_fusion.5
  516.7 0.9 bitcast_convert_fusion.5
  517.7 2.0 convert_add_fusion.5
  520.7 2.0 convert_add_fusion.5
  523.6 2.0 convert_add_fusion.5
  525.7 0.9 bitcast_convert_fusion.5
  526.6 2.0 convert_add_fusion.5
  528.6 0.9 bitcast_convert_fusion.5
  529.6 2.0 convert_add_fusion.5
  531.6 0.9 bitcast_convert_fusion.5
  532.6 2.0 convert_add_fusion.5
  534.6 0.9 bitcast_convert_fusion.5
  535.5 2.0 convert_add_fusion.5
  537.6 0.9 bitcast_convert_fusion.5
  538.5 2.0 convert_add_fusion.5
  541.5 2.0 convert_add_fusion.5
  544.5 2.0 convert_add_fusion.5
  546.5 0.9 bitcast_convert_fusion.5
  547.4 2.0 convert_add_fusion.5
  549.5 0.9 bitcast_convert_fusion.5
  550.4 2.0 convert_add_fusion.5
  552.4 0.9 bitcast_convert_fusion.5
  553.4 2.0 convert_add_fusion.5
  555.4 0.9 bitcast_convert_fusion.5
  556.3 2.0 convert_add_fusion.5
  559.3 2.0 convert_add_fusion.5
  562.3 2.0 convert_add_fusion.5
  564.3 0.9 bitcast_convert_fusion.5
  565.3 2.0 convert_add_fusion.5
  567.3 0.9 bitcast_convert_fusion.5
  568.2 2.0 convert_add_fusion.5
  571.2 2.0 convert_add_fusion.5
  574.2 2.0 convert_add_fusion.5
  577.2 2.0 convert_add_fusion.5
  580.1 2.0 convert_add_fusion.5
  583.1 2.0 convert_add_fusion.5
  586.1 2.0 convert_add_fusion.5
  588.4 1.0 copy.48
  (48 shorter events, 17.2 us)
Async XLA Ops:
  7.2 279.1 %copy-start = (bf16[1,512,2,512]{3,2,1,0:T(2,128)(2,1)S(1)}, bf16[1,512,2,512]{3,2,1,0:T(2,128)(2,1)}, u32[]{:S(2)}) copy-start(bf16[1,512,2,512]{3,2,1,0:T(2,128)(2,1)} %param.15) | copy-start | bytes 3145732
  7.2 105.5 %all-gather.6.cloned.1.call-start = ((), (), s32[]{:S(2)}) async-start(), calls=%async_computation.1 | async-start | bytes 8650752 | tf_op jit(solution)/shard_map/all_gather | solution.py:14
  9.1 263.6 %all-gather.8.cloned.1.call-start = ((), (), s32[]{:S(2)}) async-start(), calls=%async_computation.2 | async-start | bytes 2359296 | tf_op jit(solution)/shard_map/all_gather | solution.py:72
  112.8 0.7 copy-start.2
  112.8 1.6 copy-start.4
  114.3 254.7 %reduce-scatter.2.cloned.1.call-start = ((), (), s32[]{:S(2)}) async-start(), calls=%async_computation.3 | async-start | bytes 2359296 | tf_op jit(solution)/shard_map/reduce_scatter | solution.py:76
  118.6 167.5 %copy-start.3 = (f32[2,2,128]{2,1,0:T(2,128)S(1)}, f32[2,2,128]{2,1,0:T(2,128)}, u32[]{:S(2)}) copy-start(f32[2,2,128]{2,1,0:T(2,128)} %param.16) | copy-start | bytes 6148
  118.6 167.7 %copy-start.1 = (bf16[512,2,128]{0,2,1:T(8,128)(2,1)S(1)}, bf16[512,2,128]{0,2,1:T(8,128)(2,1)}, u32[]{:S(2)}) copy-start(bf16[512,2,128]{0,2,1:T(8,128)(2,1)} %fusion.19) | copy-start | bytes 786436
  286.0 188.7 %all-gather.10.cloned.1.call-start = ((), (), s32[]{:S(2)}) async-start(), calls=%async_computation.4 | async-start | bytes 8650752 | tf_op jit(solution)/shard_map/all_gather | solution.py:14
Sparse Core Ops, SparseCore 0:
  11.2 101.4 all-gather.5
  115.0 157.6 all-gather.7
  286.1 34.6 reduce-scatter.1
  371.3 103.2 all-gather.9
where the time goes:
time: 598 us; the launch traced here: 596 us
  waiting for transfers between devices  303 us (51%)
  blocking collectives  131 us (22%)
  other arithmetic  92.9 us (16%)
  local copies, waits for them, and re-layouts  31.4 us (5%)
  matrix products  22.2 us (4%)
  between operations  14 us (2%)
    all_gather x1, waiting for transfers between devices, on_device(): lax.all_gather(forward_b, 'space', axis=0, tiled=True)  154 us
    all_gather x2, waiting for transfers between devices, carried_in(): lax.all_gather(a.astype(kind), axis)  149 us
    psum x1, blocking collectives, on_device(): fixed_forward = lax.psum(contrib, ('tm', 'space')).astype(jnp.bfloat16)  78.9 us
    add x31, other arithmetic, combine(): value_l + latter[0] * value_e  62.3 us
    all_gather x1, blocking collectives, carried_in(): lax.all_gather(a.astype(kind), axis)  52.1 us
    convert_element_type x31, other arithmetic, one(): lax.dynamic_index_in_dim(a, source, 0, False).astype(own.dtype)  28.8 us
    while x4, local copies, waits for them, and re-layouts, carried_in(): return lax.fori_loop(0, ahead, one, state)  24.8 us
    dot_general x1, matrix products, on_device(): jnp.einsum('hrn,rhk->nhk', block, inner_rows, preferred_element_type=jnp....  13.2 us
  transfers between devices with their start and end apart: 4, of which 3 were waited for; matrix products, arithmetic and copies ran while one was open for 2% of the time, Pallas kernels for 0%

commit v1 on v0

--- a/solution.py
+++ b/solution.py
@@ -69,7 +69,9 @@
     inner_rows = jnp.einsum(
         "hrn,nhk->rhk",
         block,
-        lax.all_gather(forward_b, "space", axis=0, tiled=True),
+        jnp.concatenate(
+            lax.all_to_all(jnp.stack([forward_b] * lax.axis_size("space")), "space", 0, 0), axis=0
+        ),
         preferred_element_type=jnp.float32,
     ).astype(jnp.bfloat16)
     block = masked_rows

time: 598 us -> 602 us (level)
  waiting for transfers between devices: 303 us -> 169 us
  blocking collectives: 131 us -> 263 us
    all_gather x1 -> x0, waiting for transfers between devices: 154 us -> none  [on_device(): lax.all_gather(forward_b, 'space', axis=0, tiled=True)]
    psum x1, blocking collectives: 78.9 us -> 211 us  [on_device(): fixed_forward = lax.psum(contrib, ('tm', 'space')).astype(jnp.bfloat16)]
    all_to_all x0 -> x1, waiting for transfers between devices: none -> 21.5 us  [on_device(): lax.all_to_all(jnp.stack([forward_b] * lax.axis_size('space')), 'space',...]
where the time goes in v1:
time: 602 us; the launch traced here: 599 us
  blocking collectives  263 us (44%)
  waiting for transfers between devices  169 us (28%)
  other arithmetic  92.1 us (15%)
  local copies, waits for them, and re-layouts  34.6 us (6%)
  matrix products  20.7 us (3%)
  between operations  13.9 us (2%)
    psum x1, blocking collectives, on_device(): fixed_forward = lax.psum(contrib, ('tm', 'space')).astype(jnp.bfloat16)  211 us
    all_gather x2, waiting for transfers between devices, carried_in(): lax.all_gather(a.astype(kind), axis)  147 us
    add x31, other arithmetic, combine(): value_l + latter[0] * value_e  62.3 us
    all_gather x1, blocking collectives, carried_in(): lax.all_gather(a.astype(kind), axis)  52.1 us
    convert_element_type x31, other arithmetic, one(): lax.dynamic_index_in_dim(a, source, 0, False).astype(own.dtype)  28.7 us
    while x4, local copies, waits for them, and re-layouts, carried_in(): return lax.fori_loop(0, ahead, one, state)  24.8 us
    all_to_all x1, waiting for transfers between devices, on_device(): lax.all_to_all(jnp.stack([forward_b] * lax.axis_size('space')), 'space',...  21.5 us
    dot_general x1, matrix products, on_device(): jnp.einsum('hrn,rhk->nhk', block, inner_rows, preferred_element_type=jnp....  13.3 us
  transfers between devices with their start and end apart: 4, of which 3 were waited for; matrix products, arithmetic and copies ran while one was open for 2% of the time, Pallas kernels for 0%

profile of v1, /device:TPU:2, one launch (start us, length us, event | category | flops | bytes accessed | tf_op | source)
XLA Modules:
  0.0 599.3 jit_solution(3085925063111540936)
XLA Ops:
  7.2 1.9 copy.81
  9.1 1.2 copy.51
  11.1 52.1 %all-gather = bf16[32,512,2]{1,2,0:T(2,128)(2,1)S(1)} all-gather(bf16[1,512,2]{1,2,0:T(2,128)(2,1)S(1)} %convert_element_type.103), channel_id=2, replica_groups=mesh['tm'=32,'space'=8] {'tm'}, dimensions={0}, use_global_device_ids=true | all-gather | bytes 67584 | tf_op jit(solution)/shard_map/all_gather | solution.py:14
  63.2 3.3 copy.54
  66.5 46.1 %all-gather.5.cloned.1.call-done = bf16[32,512,2,128]{3,1,2,0:T(8,128)(2,1)} async-done(((bf16[1,512,2,128]{3,1,2,0:T(8,128)(2,1)}), bf16[32,512,2,128]{3,1,2,0:T(8,128)(2,1)}) %all-gather.5.cloned.1.call-update) | async-done | bytes 8388624 | tf_op jit(solution)/shard_map/all_gather | solution.py:14
  113.6 1.5 stack.2
  115.1 4.8 all-to-all-start
  120.0 4.2 fusion
  124.1 21.5 %all-to-all-done = bf16[8,512,2,128]{1,3,2,0:T(8,128)(2,1)S(1)} async-done(((bf16[8,512,2,128]{1,3,2,0:T(8,128)(2,1)}), bf16[8,512,2,128]{1,3,2,0:T(8,128)(2,1)S(1)}, u32[]{:S(2)}, u32[]{:S(2)}) %all-to-all-start) | async-done | bytes 2097184 | tf_op jit(solution)/shard_map/all_to_all | solution.py:73
  145.7 1.6 copy.72
  147.3 13.3 %fusion.4 = bf16[4096,2,128]{0,2,1:T(8,128)(2,1)} fusion(bf16[2,1,512,4096]{3,2,1,0:T(8,128)(2,1)} %param.11, pred[512,4096]{1,0:T(8,128)(4,1)} %fusion, bf16[4096,2,128]{0,2,1:T(8,128)(2,1)} %bitcast.78), kind=kOutput, calls=%fused_computation.12 | convolution fusion | flops 2157051904 | bytes 14680064 | tf_op jit(solution)/shard_map/hrn,rhk->nhk/dot_general | solution.py:79
  161.3 1.1 dynamic_update_slice.3
  162.4 211.2 %all-reduce.1 = bf16[2,512,128]{1,2,0:T(8,128)(2,1)S(1)} all-reduce(f32[2,512,128]{1,2,0:T(8,128)S(1)} %dynamic_update_slice.3), channel_id=1, replica_groups=mesh['tm'=32,'space'=8] {'tm','space'}, use_global_device_ids=true, to_apply=%region_3.4 | all-reduce | flops 131072 | bytes 786432 | tf_op jit(solution)/shard_map/psum | solution.py:93
  374.5 2.1 multiply_convert_fusion
  377.2 100.9 %all-gather.7.cloned.1.call-done = bf16[16384,2,128]{0,2,1:T(8,128)(2,1)} async-done(((bf16[512,2,128]{0,2,1:T(8,128)(2,1)}), bf16[16384,2,128]{0,2,1:T(8,128)(2,1)}) %all-gather.7.cloned.1.call-update) | async-done | bytes 8388624 | tf_op jit(solution)/shard_map/all_gather | solution.py:14
  478.1 21.1 %copy.70 = bf16[16384,2,128]{2,1,0:T(2,128)(2,1)} copy(bf16[16384,2,128]{0,2,1:T(8,128)(2,1)} %all-gather.7.cloned.1.call-done) | data formatting | bytes 16777216 | tf_op jit(solution)/shard_map/while | solution.py:29
  499.3 92.2 %while.27 = (s32[]{:T(128)}, f32[512,2,128]{2,1,0:T(2,128)S(1)}, s32[]{:T(128)}, bf16[32,512,2,128]{3,2,1,0:T(2,128)(2,1)}, bf16[32,512,2,1]{2,1,3,0:T(8,128)(2,...) while((s32[]{:T(128)}, f32[512,2,128]{2,1,0:T(2,128)S(1)}, s32[]{:T(128)}, ...), condition=%wide.region_5.6_spmd, body=%wide.region_4.5_spmd.sunk | while | flops 394246 | bytes 1321107 | solution.py:29
  499.4 0.9 bitcast_convert_fusion.5
  500.3 2.0 convert_add_fusion.5
  502.3 0.9 bitcast_convert_fusion.5
  503.3 2.0 convert_add_fusion.5
  505.3 0.9 bitcast_convert_fusion.5
  506.2 2.0 convert_add_fusion.5
  509.2 2.0 convert_add_fusion.5
  511.3 0.9 bitcast_convert_fusion.5
  512.2 2.0 convert_add_fusion.5
  515.2 2.0 convert_add_fusion.5
  518.1 2.0 convert_add_fusion.5
  520.2 0.9 bitcast_convert_fusion.5
  521.1 2.0 convert_add_fusion.5
  524.1 2.0 convert_add_fusion.5
  526.1 0.9 bitcast_convert_fusion.5
  527.1 2.0 convert_add_fusion.5
  530.0 2.0 convert_add_fusion.5
  532.1 0.9 bitcast_convert_fusion.5
  533.0 2.0 convert_add_fusion.5
  536.0 2.0 convert_add_fusion.5
  538.9 2.0 convert_add_fusion.5
  541.0 0.9 bitcast_convert_fusion.5
  541.9 2.0 convert_add_fusion.5
  544.9 2.0 convert_add_fusion.5
  546.9 0.9 bitcast_convert_fusion.5
  547.9 2.0 convert_add_fusion.5
  550.8 2.0 convert_add_fusion.5
  552.9 0.9 bitcast_convert_fusion.5
  553.8 2.0 convert_add_fusion.5
  556.8 2.0 convert_add_fusion.5
  559.8 2.0 convert_add_fusion.5
  561.8 0.9 bitcast_convert_fusion.5
  562.7 2.0 convert_add_fusion.5
  565.7 2.0 convert_add_fusion.5
  567.7 0.9 bitcast_convert_fusion.5
  568.7 2.0 convert_add_fusion.5
  571.6 2.0 convert_add_fusion.5
  574.6 2.0 convert_add_fusion.5
  576.7 0.9 bitcast_convert_fusion.5
  577.6 2.0 convert_add_fusion.5
  580.6 2.0 convert_add_fusion.5
  582.6 0.9 bitcast_convert_fusion.5
  583.5 2.0 convert_add_fusion.5
  586.5 2.0 convert_add_fusion.5
  588.6 0.9 bitcast_convert_fusion.5
  589.5 2.0 convert_add_fusion.5
  591.8 1.0 copy.66
  (49 shorter events, 19.1 us)
Async XLA Ops:
  7.2 153.7 %copy-start = (bf16[1,512,2,512]{3,2,1,0:T(2,128)(2,1)S(1)}, bf16[1,512,2,512]{3,2,1,0:T(2,128)(2,1)}, u32[]{:S(2)}) copy-start(bf16[1,512,2,512]{3,2,1,0:T(2,128)(2,1)} %param.15) | copy-start | bytes 3145732
  7.2 105.5 %all-gather.5.cloned.1.call-start = ((), (), s32[]{:S(2)}) async-start(), calls=%async_computation.2 | async-start | bytes 8650752 | tf_op jit(solution)/shard_map/all_gather | solution.py:14
  112.8 0.7 copy-start.1
  113.0 6.9 %copy-start.4 = (s32[32,32]{1,0:T(8,128)S(1)}, s32[32,32]{1,0:T(8,128)}, u32[]{:S(2)}) copy-start(s32[32,32]{1,0:T(8,128)} %param.12) | copy-start | bytes 12292
  115.1 30.6 %all-to-all-start = ((bf16[8,512,2,128]{1,3,2,0:T(8,128)(2,1)}), bf16[8,512,2,128]{1,3,2,0:T(8,128)(2,1)S(1)}, u32[]{:S(2)}, u32[]{:S(2)}) async-start(bf16[8,512,2,128]{1,3,2,0:T(8,128)(2,1)} %stack.2), calls=%async_computation | async-start | bytes 4194304 | tf_op jit(solution)/shard_map/all_to_all | solution.py:73
  119.9 254.5 %reduce-scatter.2.cloned.1.call-start = ((), (), s32[]{:S(2)}) async-start(), calls=%async_computation.3 | async-start | bytes 2359296 | tf_op jit(solution)/shard_map/reduce_scatter | solution.py:78
  147.3 13.4 %copy-start.2 = (f32[2,2,128]{2,1,0:T(2,128)S(1)}, f32[2,2,128]{2,1,0:T(2,128)}, u32[]{:S(2)}) copy-start(f32[2,2,128]{2,1,0:T(2,128)} %param.16) | copy-start | bytes 6148
  160.6 213.1 %copy-start.3 = (bf16[2,512,512]{2,1,0:T(8,128)(2,1)S(1)}, bf16[2,512,512]{2,1,0:T(8,128)(2,1)}, u32[]{:S(2)}) copy-start(bf16[2,512,512]{2,1,0:T(8,128)(2,1)} %param.17) | copy-start | bytes 3145732
  160.6 317.5 %all-gather.7.cloned.1.call-start = ((), (), s32[]{:S(2)}) async-start(), calls=%async_computation.4 | async-start | bytes 8650752 | tf_op jit(solution)/shard_map/all_gather | solution.py:14
Sparse Core Ops, SparseCore 0:
  11.2 101.4 all-gather.4
  160.7 163.8 reduce-scatter.1
  376.8 101.3 all-gather.6
